TPU v7x, 256 devices: a whole 4x4x8 slice. The times are simulated.
256 devices in a mesh: expert: 64 (over x, z, core), tensor: 4 (over y).
Axes of the slice: x: 4, y: 4, z: 8, core: 2. Of those that a mesh axis runs over, the one named last changes fastest.
Arguments:
- tokens: bfloat16 [4096, 7168], P('expert', 'tensor'), may hold values from -48 to 48
- expert_ids: int32 [4096, 8], P('expert'), may hold values from 0 to 63, all different within a row; in each aligned block of 64 rows (0 to 63, 64 to 127, ...) at most 12 rows name the same one
- route_weights: float32 [4096, 8], P('expert'), may hold values from 0.02 to 0.2
- gate_weight: bfloat16 [64, 7168, 1024], P('expert', None, 'tensor'), may hold values from -0.0625 to 0.0625
- up_weight: bfloat16 [64, 7168, 1024], P('expert', None, 'tensor'), may hold values from -0.0625 to 0.0625
- down_weight: bfloat16 [64, 1024, 7168], P('expert', 'tensor'), may hold values from -0.1875 to 0.1875
Outputs:
- layer_out: bfloat16 [4096, 7168], P('expert', 'tensor')
- scales: float32 [7168], P('tensor')
Inputs may be any that keep to these rules, and one draw needn't show every extreme that they name: `expert_ids`: each row names 8 different experts. Among the 64 rows of one index of expert (aligned blocks of rows) no expert is named by more than 12 rows, and in every draw some expert is named by exactly 12 rows of some block.
All inputs are finite; a program needn't handle non-finite values.
Results may differ from a plain program's by a relative error of at most 0.015.
Values may be sent and summed in bfloat16 or wider, within the bound.
A program may use at most 128 MiB of HBM per device.

v0:
```python
import jax
import jax.numpy as jnp
from jax import lax
from jax.sharding import PartitionSpec as P

EPS = 1e-05
CLIP_SHARE = 0.5


def routing_tables(expert_ids, expert_count, capacity):
    tok_count, top_count = expert_ids.shape
    flat_ids = expert_ids.reshape(-1)
    onehot = (flat_ids[:, None] == jnp.arange(expert_count, dtype=jnp.int32)[None, :]).astype(
        jnp.int32
    )
    before = jnp.cumsum(onehot, axis=0) - onehot
    position = jnp.sum(before * onehot, axis=1)
    target = flat_ids * capacity + position
    source = jnp.arange(tok_count * top_count, dtype=jnp.int32) // top_count
    return (target, source)


def pack_rows(rows, target, source, buffer_rows):
    return jnp.zeros((buffer_rows, rows.shape[1]), rows.dtype).at[target].set(rows[source])


def scale_terms(act_max, wt_max):
    scales = jnp.sqrt((act_max + EPS) / (wt_max + EPS))
    clip_limit = CLIP_SHARE * jnp.max(act_max / scales)
    return (scales, clip_limit)


def on_device(tokens, expert_ids, route_weights, gate_weight, up_weight, down_weight):
    expert_count = lax.axis_size("expert")
    tok_count, part_width = tokens.shape
    top_count = expert_ids.shape[1]
    capacity = min(tok_count, 3 * tok_count * top_count // (2 * expert_count))
    buffer_rows = expert_count * capacity
    target, source = routing_tables(expert_ids, expert_count, capacity)
    w_local = jnp.maximum(
        jnp.max(jnp.abs(gate_weight[0]), axis=1), jnp.max(jnp.abs(up_weight[0]), axis=1)
    ).astype(jnp.float32)
    a_local = jnp.max(jnp.abs(tokens), axis=0).astype(jnp.float32)
    a_part = lax.pmax(a_local, "expert")
    wt_max = lax.pmax(w_local, ("expert", "tensor"))
    act_max = lax.all_gather(a_part, "tensor", axis=0, tiled=True)
    scales, clip_limit = scale_terms(act_max, wt_max)
    own_scales = lax.dynamic_slice_in_dim(scales, lax.axis_index("tensor") * part_width, part_width)
    smooth_part = jnp.clip(tokens.astype(jnp.float32) / own_scales, -clip_limit, clip_limit).astype(
        jnp.bfloat16
    )
    full_rows = lax.all_gather(smooth_part, "tensor", axis=1, tiled=True)
    packed = pack_rows(full_rows, target, source, buffer_rows)
    smoothed = lax.all_to_all(packed, "expert", split_axis=0, concat_axis=0, tiled=True)
    gate_folded = (scales[:, None] * gate_weight[0].astype(jnp.float32)).astype(jnp.bfloat16)
    up_folded = (scales[:, None] * up_weight[0].astype(jnp.float32)).astype(jnp.bfloat16)
    gate_act = jnp.dot(smoothed, gate_folded, preferred_element_type=jnp.float32)
    up_act = jnp.dot(smoothed, up_folded, preferred_element_type=jnp.float32)
    hidden = (jax.nn.silu(gate_act) * up_act).astype(jnp.bfloat16)
    down_local = down_weight[0]
    summed = lax.psum_scatter(
        lax.dot_general(
            down_local, hidden, (((0,), (1,)), ((), ())), preferred_element_type=jnp.float32
        ).astype(jnp.bfloat16),
        "tensor",
        scatter_dimension=0,
        tiled=True,
    )
    returned = lax.all_to_all(summed, "expert", split_axis=1, concat_axis=1, tiled=True)
    picked_cols = returned[:, target].reshape(part_width, tok_count, top_count)
    mixed = jnp.einsum("dtk,tk->td", picked_cols.astype(jnp.float32), route_weights)
    own_part = lax.dynamic_slice_in_dim(scales, lax.axis_index("tensor") * part_width, part_width)
    return (mixed.astype(jnp.bfloat16), own_part)


def solution(mesh):
    placed = (
        P("expert", "tensor"),
        P("expert", None),
        P("expert", None),
        P("expert", None, "tensor"),
        P("expert", None, "tensor"),
        P("expert", "tensor", None),
    )
    return jax.shard_map(
        on_device,
        mesh=mesh,
        in_specs=placed,
        out_specs=(P("expert", "tensor"), P("tensor")),
        check_vma=False,
    )
```

profile of v0, /device:TPU:1, one launch (start us, length us, event | category | flops | bytes accessed | tf_op | source)
XLA Modules:
  0.0 892.5 jit_solution(10466719098032497252)
XLA Ops:
  7.2 0.8 copy.13
  8.2 0.7 broadcast_multiply_fusion
  8.9 5.2 abs_reduce_fusion
  14.1 81.6 %pmax.15 = f32[7168]{0:T(1024)S(1)} all-reduce(f32[7168]{0:T(1024)S(1)} %maximum_convert_fusion), channel_id=1, replica_groups=mesh['expert'=64,'tensor'=4] {'expert','tensor'}, use_global_device_ids=true, to_apply=%region_7.8 | all-reduce | flops 7168 | bytes 57344 | tf_op jit(solution)/shard_map/pmax | solution.py:45
  95.7 126.3 %pmax.14 = f32[1792]{0:T(1024)S(1)} all-reduce(bf16[1792]{0:T(1024)(128)(2,1)S(1)} %abs_reduce_fusion.2), channel_id=1, replica_groups=mesh['expert'=64,'tensor'=4] {'expert'}, use_global_device_ids=true, to_apply=%region_4.5 | all-reduce | flops 1792 | bytes 10752 | tf_op jit(solution)/shard_map/pmax | solution.py:44
  222.0 9.1 %all-gather = f32[4,1,1792]{2,1,0:T(1,128)S(1)} all-gather(f32[1,1,1792]{2,1,0:T(1,128)S(1)} %reshape.141), channel_id=1, replica_groups=mesh['expert'=64,'tensor'=4] {'tensor'}, dimensions={0}, use_global_device_ids=true | all-gather | bytes 35840 | tf_op jit(solution)/shard_map/all_gather | solution.py:46
  231.1 0.6 divide_reduce_fusion
  232.6 11.3 %all_gather.7 = bf16[64,7168]{1,0:T(8,128)(2,1)S(1)} all-gather(bf16[64,1792]{1,0:T(8,128)(2,1)S(1)} %minimum_convert_fusion), channel_id=1, replica_groups=mesh['expert'=64,'tensor'=4] {'tensor'}, dimensions={1}, use_global_device_ids=true | all-gather | bytes 1146880 | tf_op jit(solution)/shard_map/all_gather | solution.py:52
  243.9 1.2 reduce-window.6
  245.6 7.0 gather_fusion
  252.8 27.9 %scatter_custom_fusion = bf16[768,7168]{1,0:T(8,128)(2,1)} fusion(s32[512]{0:T(512)S(1)} %bitcast.59, bf16[512,7168]{1,0:T(8,128)(2,1)} %gather_fusion, bf16[]{:T(256)} %constant.17.clone.1), kind=kCustom, calls=%fused_computation.7 | custom fusion | bytes 11010560 | tf_op jit(solution)/shard_map/scatter | solution.py:24
  280.7 15.3 %all_to_all.16 = bf16[64,12,7168]{2,1,0:T(8,128)(2,1)} reshape(bf16[768,7168]{1,0:T(8,128)(2,1)} %scatter_custom_fusion) | data formatting | bytes 22020096 | tf_op jit(solution)/shard_map/all_to_all | solution.py:54
  296.0 333.2 %all_to_all.24 = bf16[64,12,7168]{2,1,0:T(8,128)(2,1)} all-to-all(bf16[64,12,7168]{2,1,0:T(8,128)(2,1)} %all_to_all.16), channel_id=1, replica_groups=mesh['expert'=64,'tensor'=4] {'expert'}, dimensions={0} | all-to-all | bytes 22020096 | tf_op jit(solution)/shard_map/all_to_all | solution.py:54
  629.2 15.9 %all_to_all.18 = bf16[768,7168]{1,0:T(8,128)(2,1)} reshape(bf16[64,12,7168]{2,1,0:T(8,128)(2,1)} %all_to_all.24) | data formatting | bytes 22020096 | tf_op jit(solution)/shard_map/all_to_all | solution.py:54
  645.1 8.3 fusion.4
  653.4 21.9 %fusion = bf16[7168,768]{0,1:T(8,128)(2,1)} fusion(bf16[1,256,7168]{2,1,0:T(8,128)(2,1)} %param.11, bf16[768,7168]{1,0:T(8,128)(2,1)} %all_to_all.18, bf16[1,7168,256]{2,1,0:T(8,128)(2,1)} %param.10, f32[7168]{0:T(1024)S(1)} %get-tuple-element.3, f32[768,256]{1,0:T(8,128)S(1)} %fusion.4), kind=kOutput, calls=%fused_computation.4 | convolution fusion | flops 5649334272 | bytes 30175232 | tf_op jit(solution)/shard_map/dot_general | solution.py:62
  675.3 99.5 %reduce-scatter.2.cloned.1.call-done = bf16[1792,768]{0,1:T(8,128)(2,1)} async-done(((bf16[7168,768]{0,1:T(8,128)(2,1)}), bf16[1792,768]{0,1:T(8,128)(2,1)}) %reduce-scatter.2.cloned.1.call-update) | async-done | bytes 2752528 | tf_op jit(solution)/shard_map/reduce_scatter | solution.py:61
  774.7 5.3 all_to_all.19
  780.1 10.9 %all-to-all-start.1 = ((bf16[1792,64,12]{0,2,1:T(8,128)(2,1)}), bf16[1792,64,12]{0,2,1:T(8,128)(2,1)}, u32[]{:S(2)}, u32[]{:S(2)}) async-start(bf16[1792,64,12]{0,2,1:T(8,128)(2,1)} %all_to_all.19), calls=%async_computation.2 | async-start | bytes 7340032 | tf_op jit(solution)/shard_map/all_to_all | solution.py:69
  791.1 84.5 %all-to-all-done.1 = bf16[1792,64,12]{0,2,1:T(8,128)(2,1)} async-done(((bf16[1792,64,12]{0,2,1:T(8,128)(2,1)}), bf16[1792,64,12]{0,2,1:T(8,128)(2,1)}, u32[]{:S(2)}, u32[]{:S(2)}) %all-to-all-start.1) | async-done | bytes 2752544 | tf_op jit(solution)/shard_map/all_to_all | solution.py:69
  875.6 3.8 all_to_all.21
  879.4 3.2 gather_fusion.1
  882.6 2.1 fusion.12
  884.7 0.7 copy.21
  (27 shorter events, 1.2 us)
Async XLA Ops:
  7.2 88.5 %copy-start = (bf16[64,1792]{1,0:T(8,128)(2,1)S(1)}, bf16[64,1792]{1,0:T(8,128)(2,1)}, u32[]{:S(2)}) copy-start(bf16[64,1792]{1,0:T(8,128)(2,1)} %param.6) | copy-start | bytes 688132
  7.2 767.6 %reduce-scatter.2.cloned.1.call-start = ((), (), s32[]{:S(2)}) async-start(), calls=%async_computation.3 | async-start | bytes 13762560 | tf_op jit(solution)/shard_map/reduce_scatter | solution.py:61
  232.5 20.1 %copy-start.1 = (f32[1792]{0:T(1024)}, f32[1792]{0:T(1024)S(1)}, u32[]{:S(2)}) copy-start(f32[1792]{0:T(1024)S(1)} %dynamic_slice.4) | copy-start | bytes 21508
  675.3 115.7 %copy-start.2 = (f32[64,8]{0,1:T(8,128)S(1)}, f32[64,8]{0,1:T(8,128)}, u32[]{:S(2)}) copy-start(f32[64,8]{0,1:T(8,128)} %param.8) | copy-start | bytes 6148
  780.1 95.5 %all-to-all-start.1 = ((bf16[1792,64,12]{0,2,1:T(8,128)(2,1)}), bf16[1792,64,12]{0,2,1:T(8,128)(2,1)}, u32[]{:S(2)}, u32[]{:S(2)}) async-start(bf16[1792,64,12]{0,2,1:T(8,128)(2,1)} %all_to_all.19), calls=%async_computation.2 | async-start | bytes 7340032 | tf_op jit(solution)/shard_map/all_to_all | solution.py:69
Sparse Core Ops, SparseCore 0:
  675.4 99.3 reduce-scatter.1
where the time goes:
time: 900 us; the launch traced here: 892 us
  blocking collectives  561 us (62%)
  waiting for transfers between devices  184 us (20%)
  local copies, waits for them, and re-layouts  80.8 us (9%)
  matrix products  32.3 us (4%)
  between operations  15.1 us (2%)
  starting transfers between devices  10.9 us (1%)
    all_to_all x1, blocking collectives, on_device(): lax.all_to_all(packed, 'expert', split_axis=0, concat_axis=0, tiled=True)  333 us
    pmax x1, blocking collectives, on_device(): a_part = lax.pmax(a_local, 'expert')  126 us
    reduce_scatter x1, waiting for transfers between devices, on_device(): lax.psum_scatter(lax.dot_general(down_local, hidden, (((0,), (1,)), ((),...  99.5 us
    all_to_all x1, waiting for transfers between devices, on_device(): lax.all_to_all(summed, 'expert', split_axis=1, concat_axis=1, tiled=True)  84.5 us
    pmax x1, blocking collectives, on_device(): wt_max = lax.pmax(w_local, ('expert', 'tensor'))  81.6 us
    all_to_all x2, local copies, waits for them, and re-layouts, on_device(): lax.all_to_all(packed, 'expert', split_axis=0, concat_axis=0, tiled=True)  31.3 us
    scatter x1, local copies, waits for them, and re-layouts, pack_rows(): jnp.zeros((buffer_rows, rows.shape[1]), rows.dtype).at[target]  27.9 us
    dot_general x1, matrix products, on_device(): lax.dot_general(down_local, hidden, (((0,), (1,)), ((), ())), preferred_e...  21.9 us
  transfers between devices with their start and end apart: 2, of which 2 were waited for; matrix products, arithmetic and copies ran while one was open for 0% of the time, Pallas kernels for 0%

commit v1 on v0

v1 whole, which is shorter than its diff:
```python
import functools

import jax
import jax.numpy as jnp
import numpy as np
from jax import lax
from jax.experimental import pallas as pl
from jax.experimental.pallas import tpu as pltpu
from jax.sharding import PartitionSpec as P

EPS = 1e-05
CLIP_SHARE = 0.5
MESH = pl.DeviceIdType.MESH

NX, NZ, NC = 4, 8, 2
NG = NX * NC
NY = 4
CAP = 12
TOK = 64
TOP = 8
WIDTH = 1792
D = NY * WIDTH
HID = 256
PIECE = NZ * CAP
ROWS = NG * PIECE
STOK = NZ * TOK
CODE = 16
AUX = 128
WROWS = D // 128
AROWS = WIDTH // 128
MROWS = -(-(WROWS + AROWS) // 8) * 8
RIGHT, LEFT = NZ // 2, NZ - 1 - NZ // 2
COLT = 256
HALF = ROWS // 2


def place():
    me = lax.axis_index("expert")
    x = me // (NZ * NC)
    z = lax.rem(me // NC, NZ)
    c = lax.rem(me, NC)
    return x, z, c, lax.axis_index("tensor")


def expert_at(group, z):
    return (group // NC) * (NZ * NC) + z * NC + lax.rem(group, NC)


def enter(peers):
    barrier = pltpu.get_barrier_semaphore()
    for peer in peers:
        pl.semaphore_signal(barrier, inc=1, device_id=peer, device_id_type=MESH)
    pl.semaphore_wait(barrier, len(peers))


def neighbours():
    x, z, c, y = place()
    g = x * NC + c
    up = (expert_at(g, lax.rem(z + 1, NZ)), y)
    down = (expert_at(g, lax.rem(z + NZ - 1, NZ)), y)
    group = [(expert_at(lax.rem(g + j, NG), z), y) for j in range(1, NG)]
    me = expert_at(g, z)
    column = [(me, lax.rem(y + j, NY)) for j in range(1, NY)]
    return z, g, y, up, down, group, column


def remote(src, dst, send, recv, peer):
    return pltpu.make_async_remote_copy(
        src_ref=src, dst_ref=dst, send_sem=send, recv_sem=recv, device_id=peer, device_id_type=MESH
    )


def dispatch_kernel(
    tok_ref, aux_ref, keyrow_ref, keycol_ref, down_ref,
    rows_ref, dn_ref, comb_ref, most_ref,
    tbuf, abuf, pick, sendbuf, mx, my_ref,
    d_send, d_recv, tr_send, tr_recv, tl_send, tl_recv,
    ar_send, ar_recv, al_send, al_recv,
    x_send, x_recv, m_send, m_recv, y_send, y_recv, loc_sem,
):
    z, g, y, up, down, group, column = neighbours()
    enter([up, down] + group + column)

    own_tok = pltpu.make_async_copy(tok_ref, tbuf.at[z], loc_sem.at[0])
    own_aux = pltpu.make_async_copy(aux_ref, abuf.at[z], loc_sem.at[1])
    own_tok.start()
    own_aux.start()

    def ring(own, buf, send, recv, peer, step, way):
        slot = lax.rem(z - way * step + NZ, NZ)
        src = own if step == 0 else buf.at[slot]
        return remote(src, buf.at[slot], send.at[step], recv.at[step], peer)

    tr = [ring(tok_ref, tbuf, tr_send, tr_recv, up, i, 1) for i in range(RIGHT)]
    tl = [ring(tok_ref, tbuf, tl_send, tl_recv, down, i, -1) for i in range(LEFT)]
    ar = [ring(aux_ref, abuf, ar_send, ar_recv, up, i, 1) for i in range(RIGHT)]
    al = [ring(aux_ref, abuf, al_send, al_recv, down, i, -1) for i in range(LEFT)]
    ar[0].start()
    al[0].start()
    tr[0].start()
    tl[0].start()

    own_down = pltpu.make_async_copy(
        down_ref.at[:, pl.ds(pl.multiple_of(y * WIDTH, 128), WIDTH)], dn_ref.at[y], loc_sem.at[2]
    )
    own_down.start()
    dcopies = []
    for j in range(1, NY):
        to = lax.rem(y + j, NY)
        dcopies.append(
            remote(
                down_ref.at[:, pl.ds(pl.multiple_of(to * WIDTH, 128), WIDTH)],
                dn_ref.at[y], d_send.at[j - 1], d_recv.at[j - 1], column[j - 1],
            )
        )
    for copy in dcopies:
        copy.start()

    for i in range(RIGHT):
        ar[i].wait_recv()
        if i + 1 < RIGHT:
            ar[i + 1].start()
        if i < LEFT:
            al[i].wait_recv()
            if i + 1 < LEFT:
                al[i + 1].start()
    own_aux.wait()
    tr[0].wait_recv()
    tr[1].start()
    tl[0].wait_recv()
    if LEFT > 1:
        tl[1].start()

    @pl.loop(0, NZ)
    def _(b):
        block = abuf[b, 0:TOK, :].astype(jnp.float32)
        total = jnp.zeros((TOK, ROWS), jnp.float32)
        for k in range(TOP):
            code = block[:, k : k + 1] * CODE + block[:, TOP + k : TOP + k + 1] + (b * 1024).astype(jnp.float32)
            weight = block[:, 2 * TOP + k : 2 * TOP + k + 1]
            total = total + jnp.where(code == keyrow_ref[0:1, :], weight, 0.0)
        comb_ref[pl.ds(pl.multiple_of(b * TOK, TOK), TOK), :] = total.astype(jnp.bfloat16)

    for i in range(1, RIGHT - 1):
        tr[i].wait_recv()
        tr[i + 1].start()
        if i < LEFT:
            tl[i].wait_recv()
            if i + 1 < LEFT:
                tl[i + 1].start()

    codes = []
    for b in range(NZ):
        block = abuf[b, 0:TOK, :].astype(jnp.float32)
        code = block * CODE + pltpu.roll(block, AUX - TOP, 1) + float(b * 1024)
        codes.append(code)
    code_t = jnp.transpose(jnp.concatenate(codes, axis=0))

    for r in range(0, ROWS, 96):
        key = keycol_ref[r : r + 96, 0:1]
        hit = key == code_t[0:1, :]
        for k in range(1, TOP):
            hit = hit | (key == code_t[k : k + 1, :])
        pick[r : r + 96, :] = jnp.where(hit, 1.0, 0.0).astype(jnp.bfloat16)

    wt = abuf[0, TOK : TOK + WROWS, :].astype(jnp.float32)
    for b in range(1, NZ):
        wt = jnp.maximum(wt, abuf[b, TOK : TOK + WROWS, :].astype(jnp.float32))
    mx[g] = jnp.zeros((MROWS, 128), jnp.float32)
    mx[g, 0:WROWS, :] = wt

    tr[RIGHT - 1].wait_recv()
    own_tok.wait()

    for n in range(0, WIDTH, COLT):
        tile = tbuf[:, :, n : n + COLT].reshape(STOK, COLT)
        got = jnp.dot(pick[...], tile, preferred_element_type=jnp.float32)
        sendbuf[:, :, n : n + COLT] = got.astype(jnp.bfloat16).reshape(NG, PIECE, COLT)
        top = jnp.max(jnp.abs(tile.astype(jnp.float32)), axis=0, keepdims=True)
        for q in range(COLT // 128):
            mx[g, WROWS + n // 128 + q : WROWS + n // 128 + q + 1, :] = top[:, q * 128 : q * 128 + 128]

    mcopies = [
        remote(mx.at[g], mx.at[g], m_send.at[j], m_recv.at[j], group[j]) for j in range(NG - 1)
    ]
    xcopies = [
        remote(sendbuf.at[lax.rem(g + j + 1, NG)], rows_ref.at[g], x_send.at[j], x_recv.at[j], group[j])
        for j in range(NG - 1)
    ]
    own_rows = pltpu.make_async_copy(sendbuf.at[g], rows_ref.at[g], loc_sem.at[3])
    for copy in mcopies:
        copy.start()
    for copy in xcopies:
        copy.start()
    own_rows.start()
    for copy in mcopies:
        copy.wait_recv()
    most = mx[0]
    for j in range(1, NG):
        most = jnp.maximum(most, mx[j])
    my_ref[y] = most
    ycopies = [
        remote(my_ref.at[y], my_ref.at[y], y_send.at[j], y_recv.at[j], column[j]) for j in range(NY - 1)
    ]
    for copy in ycopies:
        copy.start()
    for copy in ycopies + dcopies:
        copy.wait()
    most_ref[...] = my_ref[...]
    for copy in xcopies:
        copy.wait()
    for copy in mcopies + tr + tl + ar + al:
        copy.wait_send()
    own_rows.wait()
    own_down.wait()


def dispatch(tokens, aux, keyrow, keycol, down_local):
    vmem = pl.BlockSpec(memory_space=pltpu.VMEM)
    anyspace = pl.BlockSpec(memory_space=pl.ANY)
    dma = pltpu.SemaphoreType.DMA
    bf, f32 = jnp.bfloat16, jnp.float32
    return pl.pallas_call(
        dispatch_kernel,
        out_shape=(
            jax.ShapeDtypeStruct((NG, PIECE, WIDTH), bf),
            jax.ShapeDtypeStruct((NY, HID, WIDTH), bf),
            jax.ShapeDtypeStruct((STOK, ROWS), bf),
            jax.ShapeDtypeStruct((NY, MROWS, 128), f32),
        ),
        in_specs=[vmem, vmem, vmem, vmem, anyspace],
        out_specs=(anyspace, anyspace, vmem, vmem),
        scratch_shapes=[
            pltpu.VMEM((NZ, TOK, WIDTH), bf),
            pltpu.VMEM((NZ, AUX, 128), bf),
            pltpu.VMEM((ROWS, STOK), bf),
            pltpu.VMEM((NG, PIECE, WIDTH), bf),
            pltpu.VMEM((NG, MROWS, 128), f32),
            pltpu.VMEM((NY, MROWS, 128), f32),
            dma((NY - 1,)), dma((NY - 1,)),
            dma((RIGHT,)), dma((RIGHT,)), dma((LEFT,)), dma((LEFT,)),
            dma((RIGHT,)), dma((RIGHT,)), dma((LEFT,)), dma((LEFT,)),
            dma((NG - 1,)), dma((NG - 1,)), dma((NG - 1,)), dma((NG - 1,)),
            dma((NY - 1,)), dma((NY - 1,)), dma((4,)),
        ],
        compiler_params=pltpu.CompilerParams(
            collective_id=0, has_side_effects=True, vmem_limit_bytes=60 * 1024 * 1024
        ),
        name="dispatch",
    )(tokens, aux, keyrow, keycol, down_local)


def expert_kernel(
    rows_ref, gate_ref, up_ref, thr_ref, dn_ref, comb_ref,
    out_ref,
    xbuf, wg, wu, accg, accu, hbuf, dn, obuf, rbuf, part, rsend, rrecv, lsend, lrecv,
    yr_send, yr_recv, yl_send, yl_recv,
    hr_send, hr_recv, hl_send, hl_recv,
    x_send, x_recv, zr_send, zr_recv, zl_send, zl_recv, loc_sem,
):
    z, g, y, up, down, group, column = neighbours()
    nxt, prv = column[0], column[NY - 2]
    enter([up, down] + group + column)
    lo, hi = pl.ds(0, HALF), pl.ds(HALF, HALF)

    yr = [
        remote(rows_ref.at[lo], xbuf.at[1, lo], yr_send.at[0], yr_recv.at[0], nxt),
        remote(rows_ref.at[hi], xbuf.at[1, hi], yr_send.at[1], yr_recv.at[1], nxt),
        remote(xbuf.at[1, lo], xbuf.at[3, lo], yr_send.at[2], yr_recv.at[2], nxt),
    ]
    yl = [
        remote(rows_ref.at[hi], xbuf.at[2, hi], yl_send.at[0], yl_recv.at[0], prv),
        remote(rows_ref.at[lo], xbuf.at[2, lo], yl_send.at[1], yl_recv.at[1], prv),
        remote(xbuf.at[2, hi], xbuf.at[3, hi], yl_send.at[2], yl_recv.at[2], prv),
    ]
    for i in range(2):
        yr[i].start()
        yl[i].start()
    loads = [
        pltpu.make_async_copy(rows_ref, xbuf.at[0], loc_sem.at[0]),
        pltpu.make_async_copy(gate_ref, wg, loc_sem.at[1]),
        pltpu.make_async_copy(up_ref, wu, loc_sem.at[2]),
        pltpu.make_async_copy(dn_ref, dn, loc_sem.at[3]),
    ]
    for copy in loads:
        copy.start()
    for copy in loads:
        copy.wait()

    def add(slot, owner, start, count, first):
        krows = pl.ds(pl.multiple_of(owner * WIDTH, 256), WIDTH)
        bound = thr_ref[pl.ds(pl.multiple_of(owner * 16, 16), 16), :][0:1, :]

        @pl.loop(0, count // HALF)
        def _(i):
            sl = pl.ds(pl.multiple_of(start + i * HALF, HALF), HALF)
            x = jnp.minimum(jnp.maximum(xbuf[slot, sl, :], -bound), bound)
            a = jnp.dot(x, wg[krows, :], preferred_element_type=jnp.float32)
            b = jnp.dot(x, wu[krows, :], preferred_element_type=jnp.float32)
            if first:
                accg[sl, :] = a
                accu[sl, :] = b
            else:
                accg[sl, :] += a
                accu[sl, :] += b

    left, right, far = lax.rem(y + NY - 1, NY), lax.rem(y + 1, NY), lax.rem(y + 2, NY)
    add(0, y, 0, ROWS, True)
    yr[0].wait_recv()
    yr[2].start()
    yl[0].wait_recv()
    yl[2].start()
    add(1, left, 0, HALF, False)
    add(2, right, HALF, HALF, False)
    yr[1].wait_recv()
    add(1, left, HALF, HALF, False)
    yl[1].wait_recv()
    add(2, right, 0, HALF, False)

    def hidden(sl):
        v = accg[sl, :]
        hbuf[y, sl, :] = (v / (1.0 + jnp.exp(-v)) * accu[sl, :]).astype(jnp.bfloat16)

    hr = [
        remote(hbuf.at[y, lo], hbuf.at[y, lo], hr_send.at[0], hr_recv.at[0], nxt),
        remote(hbuf.at[y, hi], hbuf.at[y, hi], hr_send.at[1], hr_recv.at[1], nxt),
        remote(hbuf.at[left, lo], hbuf.at[left, lo], hr_send.at[2], hr_recv.at[2], nxt),
    ]
    hl = [
        remote(hbuf.at[y, lo], hbuf.at[y, lo], hl_send.at[0], hl_recv.at[0], prv),
        remote(hbuf.at[y, hi], hbuf.at[y, hi], hl_send.at[1], hl_recv.at[1], prv),
        remote(hbuf.at[right, hi], hbuf.at[right, hi], hl_send.at[2], hl_recv.at[2], prv),
    ]
    yr[2].wait_recv()
    add(3, far, 0, HALF, False)
    hidden(lo)
    hr[0].start()
    hl[0].start()
    yl[2].wait_recv()
    add(3, far, HALF, HALF, False)
    hidden(hi)
    hr[1].start()
    hl[1].start()
    hr[0].wait_recv()
    hr[2].start()
    hl[0].wait_recv()
    hl[1].wait_recv()
    hl[2].start()
    hr[1].wait_recv()
    hr[2].wait_recv()
    hl[2].wait_recv()

    @pl.loop(0, WIDTH // COLT)
    def _(i):
        cols = pl.ds(pl.multiple_of(i * COLT, COLT), COLT)
        acc = jnp.dot(hbuf[0], dn[0:HID, cols], preferred_element_type=jnp.float32)
        for q in range(1, NY):
            acc += jnp.dot(
                hbuf[q], dn[q * HID : (q + 1) * HID, cols], preferred_element_type=jnp.float32
            )
        obuf[:, cols] = acc.astype(jnp.bfloat16)

    def piece(j):
        return pl.ds(pl.multiple_of(j * PIECE, PIECE), PIECE)

    xcopies = [
        remote(obuf.at[piece(lax.rem(g + j + 1, NG))], rbuf.at[piece(g)], x_send.at[j], x_recv.at[j], group[j])
        for j in range(NG - 1)
    ]
    own = pltpu.make_async_copy(obuf.at[piece(g)], rbuf.at[piece(g)], loc_sem.at[4])
    for copy in xcopies:
        copy.start()
    own.start()
    for copy in xcopies:
        copy.wait_recv()
    own.wait()

    @pl.loop(0, WIDTH // COLT)
    def _(i):
        cols = pl.ds(pl.multiple_of(i * COLT, COLT), COLT)
        part[:, cols] = jnp.dot(comb_ref[...], rbuf[:, cols], preferred_element_type=jnp.float32)

    def of(block):
        return part[pl.ds(pl.multiple_of(lax.rem(block + 2 * NZ, NZ) * TOK, TOK), TOK), :]

    zr = [remote(rsend.at[i], rrecv.at[i], zr_send.at[i], zr_recv.at[i], up) for i in range(RIGHT)]
    zl = [remote(lsend.at[i], lrecv.at[i], zl_send.at[i], zl_recv.at[i], down) for i in range(LEFT)]
    for i in range(RIGHT):
        if i > 0:
            zr[i - 1].wait_recv()
        value = of(z + RIGHT - i)
        if i > 0:
            value = value + rrecv[i - 1].astype(jnp.float32)
        rsend[i] = value.astype(jnp.bfloat16)
        zr[i].start()
        if i < LEFT:
            if i > 0:
                zl[i - 1].wait_recv()
            value = of(z - LEFT + i)
            if i > 0:
                value = value + lrecv[i - 1].astype(jnp.float32)
            lsend[i] = value.astype(jnp.bfloat16)
            zl[i].start()
    zr[RIGHT - 1].wait_recv()
    zl[LEFT - 1].wait_recv()
    total = of(z) + rrecv[RIGHT - 1].astype(jnp.float32) + lrecv[LEFT - 1].astype(jnp.float32)
    out_ref[...] = total.astype(jnp.bfloat16)
    for copy in yr + yl + hr + hl + xcopies + zr + zl:
        copy.wait_send()


def experts(rows, gate, up, thr, dn, comb):
    vmem = pl.BlockSpec(memory_space=pltpu.VMEM)
    anyspace = pl.BlockSpec(memory_space=pl.ANY)
    dma = pltpu.SemaphoreType.DMA
    bf, f32 = jnp.bfloat16, jnp.float32
    return pl.pallas_call(
        expert_kernel,
        out_shape=jax.ShapeDtypeStruct((TOK, WIDTH), bf),
        in_specs=[anyspace, anyspace, anyspace, vmem, anyspace, vmem],
        out_specs=vmem,
        scratch_shapes=[
            pltpu.VMEM((NY, ROWS, WIDTH), bf),
            pltpu.VMEM((D, HID), bf),
            pltpu.VMEM((D, HID), bf),
            pltpu.VMEM((ROWS, HID), f32),
            pltpu.VMEM((ROWS, HID), f32),
            pltpu.VMEM((NY, ROWS, HID), bf),
            pltpu.VMEM((NY * HID, WIDTH), bf),
            pltpu.VMEM((ROWS, WIDTH), bf),
            pltpu.VMEM((ROWS, WIDTH), bf),
            pltpu.VMEM((STOK, WIDTH), f32),
            pltpu.VMEM((RIGHT, TOK, WIDTH), bf),
            pltpu.VMEM((RIGHT, TOK, WIDTH), bf),
            pltpu.VMEM((LEFT, TOK, WIDTH), bf),
            pltpu.VMEM((LEFT, TOK, WIDTH), bf),
            dma((3,)), dma((3,)), dma((3,)), dma((3,)),
            dma((3,)), dma((3,)), dma((3,)), dma((3,)),
            dma((NG - 1,)), dma((NG - 1,)),
            dma((RIGHT,)), dma((RIGHT,)), dma((LEFT,)), dma((LEFT,)),
            dma((5,)),
        ],
        compiler_params=pltpu.CompilerParams(
            collective_id=1, has_side_effects=True, vmem_limit_bytes=62 * 1024 * 1024
        ),
        name="experts",
    )(rows, gate, up, thr, dn, comb)


def on_device(tokens, expert_ids, route_weights, gate_weight, up_weight, down_weight):
    bf, f32 = jnp.bfloat16, jnp.float32
    experts_n = NG * NZ
    w_local = jnp.maximum(
        jnp.max(jnp.abs(gate_weight[0]), axis=1), jnp.max(jnp.abs(up_weight[0]), axis=1)
    ).reshape(WROWS, 128)

    named = expert_ids[:, :, None] == jnp.arange(experts_n, dtype=jnp.int32)
    chosen = jnp.any(named, axis=1).astype(bf)
    earlier = (np.arange(TOK)[:, None] > np.arange(TOK)[None, :]).astype(np.float32)
    before = jnp.dot(jnp.asarray(earlier, bf), chosen, preferred_element_type=f32)
    place_of = jnp.sum(jnp.where(named, before[:, None, :], 0.0), axis=2)
    meta = jnp.concatenate(
        [expert_ids.astype(bf), place_of.astype(bf), route_weights.astype(bf),
         jnp.zeros((TOK, 128 - 3 * TOP), bf)], axis=1)
    aux = jnp.concatenate([meta, w_local, jnp.zeros((AUX - TOK - WROWS, 128), bf)], axis=0)

    r = np.arange(ROWS)
    group, zz, p = r // PIECE, (r % PIECE) // CAP, r % CAP
    fixed = ((group // NC) * (NZ * NC) + group % NC) * CODE + p + 1024 * zz
    z = lax.rem(lax.axis_index("expert") // NC, NZ)
    key = jnp.asarray(fixed, f32) + (z * NC * CODE).astype(f32)
    keyrow = jnp.broadcast_to(key[None, :], (8, ROWS))
    keycol = jnp.broadcast_to(key[:, None], (ROWS, 128))

    rows, dn, comb, most = dispatch(tokens, aux, keyrow, keycol, down_weight[0])

    wt_max = jnp.max(most[:, :WROWS], axis=0).reshape(D)
    act_max = most[:, WROWS : WROWS + AROWS].reshape(D)
    scales = jnp.sqrt((act_max + EPS) / (wt_max + EPS))
    clip_limit = CLIP_SHARE * jnp.max(act_max / scales)
    thr = (clip_limit * scales).astype(bf).reshape(NY, 1, WIDTH)
    thr = jnp.broadcast_to(thr, (NY, 16, WIDTH)).reshape(NY * 16, WIDTH)
    out = experts(
        rows.reshape(ROWS, WIDTH), gate_weight[0], up_weight[0], thr, dn.reshape(NY * HID, WIDTH), comb
    )
    own_part = lax.dynamic_slice_in_dim(scales, lax.axis_index("tensor") * WIDTH, WIDTH)
    return (out, own_part)


def solution(mesh):
    placed = (
        P("expert", "tensor"),
        P("expert", None),
        P("expert", None),
        P("expert", None, "tensor"),
        P("expert", None, "tensor"),
        P("expert", "tensor", None),
    )
    return jax.shard_map(
        on_device,
        mesh=mesh,
        in_specs=placed,
        out_specs=(P("expert", "tensor"), P("tensor")),
        check_vma=False,
    )
```

time: 900 us -> 268 us (0.30)
  blocking collectives: 561 us -> 0 us
  Pallas kernels: 0 us -> 250 us
  waiting for transfers between devices: 184 us -> 0 us
  local copies, waits for them, and re-layouts: 80.8 us -> 4.28 us
  matrix products: 32.3 us -> 0.13 us
  between operations: 15.1 us -> 1.41 us
  starting transfers between devices: 10.9 us -> 0 us
    all_to_all x1 -> x0, blocking collectives: 333 us -> none  [on_device(): lax.all_to_all(packed, 'expert', split_axis=0, concat_axis=0, tiled=True)]
    pallas_call x0 -> x2, Pallas kernels: none -> 250 us  [the longest x1 173 us: experts(): pl.pallas_call(expert_kernel, out_shape=jax.ShapeDtypeStruct((TOK, WIDTH)...]
    pmax x2 -> x0, blocking collectives: 208 us -> none  [the longest x1 126 us: on_device(): a_part = lax.pmax(a_local, 'expert')]
    reduce_scatter x1 -> x0, waiting for transfers between devices: 99.5 us -> none  [on_device(): lax.psum_scatter(lax.dot_general(down_local, hidden, (((0,), (1,)), ((),...]
    all_to_all x1 -> x0, waiting for transfers between devices: 84.5 us -> none  [on_device(): lax.all_to_all(summed, 'expert', split_axis=1, concat_axis=1, tiled=True)]
    all_to_all x4 -> x0, local copies, waits for them, and re-layouts: 40.4 us -> none  [the longest x2 31.3 us: on_device(): lax.all_to_all(packed, 'expert', split_axis=0, concat_axis=0, tiled=True)]
    dot_general x3 -> x1, matrix products: 32.3 us -> 0.13 us  [on_device(): jnp.dot(jnp.asarray(earlier, bf), chosen, preferred_element_type=f32)]
    scatter x1 -> x0, local copies, waits for them, and re-layouts: 27.9 us -> none  [pack_rows(): jnp.zeros((buffer_rows, rows.shape[1]), rows.dtype).at[target]]
  transfers between devices with their start and end apart: 2 -> 0, of which waited for: 2 -> 0; matrix products, arithmetic and copies ran while one was open for 0% -> 0% of each run, Pallas kernels for 0% -> 0%
where the time goes in v1:
time: 268 us; the launch traced here: 267 us
  Pallas kernels  250 us (93%)
  other arithmetic  11.4 us (4%)
  local copies, waits for them, and re-layouts  4.28 us (2%)
    pallas_call x1, Pallas kernels, experts(): pl.pallas_call(expert_kernel, out_shape=jax.ShapeDtypeStruct((TOK, WIDTH)...  173 us
    pallas_call x1, Pallas kernels, dispatch(): pl.pallas_call(dispatch_kernel, out_shape=(jax.ShapeDtypeStruct((NG, PIEC...  77 us

profile of v1, /device:TPU:1, one launch (start us, length us, event | category | flops | bytes accessed | tf_op | source)
XLA Modules:
  0.0 267.5 jit_solution(6168298982335033829)
XLA Ops:
  0.7 0.1 pad.5.clone
  0.7 0.7 convert_element_type.22
  1.4 0.7 convert_element_type.20
  2.1 0.7 broadcast_add_fusion.1
  2.8 0.1 copy.17
  2.9 0.1 copy.18
  3.0 0.6 broadcast_in_dim.42.keyrow_ref
  3.6 0.0 copy-start.1
  3.6 5.2 %abs_reduce_fusion = (bf16[7168]{0:T(1024)(128)(2,1)S(1)}, bf16[7168]{0:T(1024)(128)(2,1)S(1)}) fusion(bf16[1,7168,256]{2,1,0:T(8,128)(2,1)} %param.12, bf16[1,7168,256]{2,1,0:T(8,128)(2,1)} %param.11), kind=kLoop, calls=%fused_computation | loop fusion | flops 7325696 | bytes 7368704 | tf_op jit(solution)/shard_map/reduce_max | solution.py:454
  8.8 0.0 copy-done.1
  8.8 0.1 copy.16
  8.9 0.2 fusion
  9.1 0.0 copy-done
  9.1 0.1 fusion.4
  9.2 0.2 select_reduce_fusion
  9.5 0.7 maximum_maximum_fusion.aux_ref
  10.2 0.9 broadcast_in_dim.43.keycol_ref
  11.1 77.0 %dispatch.1 = (bf16[8,96,1792]{2,1,0:T(8,128)(2,1)}, bf16[4,256,1792]{2,1,0:T(8,128)(2,1)}, bf16[512,768]{1,0:T(8,128)(2,1)}, f32[4,72,128]{2,1,0:T(8,128)}) custom-call(bf16[64,1792]{1,0:T(8,128)(2,1)} %tok_ref.1, bf16[128,128]{1,0:T(8,128)(2,1)} %maximum_maximum_fusion.aux_ref, f32[8,768]{1,0:T(8,128)} %broadcast_in_dim.42.keyrow_ref, ...), custom_call_target="tpu_custom_call" | custom-call | tf_op jit(solution)/shard_map/dispatch/pallas_call | solution.py:223
  88.2 0.9 slice_reduce_fusion
  89.1 1.4 slice_add_fusion
  91.2 0.7 fusion.1
  91.9 0.7 broadcast_in_dim.44
  92.6 173.2 %experts.1 = bf16[64,1792]{1,0:T(8,128)(2,1)} custom-call(bf16[768,1792]{1,0:T(8,128)(2,1)} %bitcast.24, bf16[7168,256]{1,0:T(8,128)(2,1)} %bitcast.21, bf16[7168,256]{1,0:T(8,128)(2,1)} %bitcast.20, bf16[64,1792]{1,0:T(8,128)(2,1)} %bitcast.25, bf16[1024,1792]{1,0:T(8,128)(2,1)} %bitcast.22, bf16[512,768]{1,0:T(8,128)(2,1)} %get-tuple-element.9.comb_ref), custom_call_target="tpu_custom_call" | custom-call | tf_op jit(solution)/shard_map/experts/pallas_call | solution.py:417
  265.8 1.6 copy.24
  (9 shorter events, 0.1 us)
Async XLA Ops:
  3.6 5.2 %copy-start.1 = (s32[64,8]{0,1:T(8,128)S(1)}, s32[64,8]{0,1:T(8,128)}, u32[]{:S(2)}) copy-start(s32[64,8]{0,1:T(8,128)} %param.9) | copy-start | bytes 6148
  3.6 5.5 %copy-start = (bf16[64,64]{1,0:T(8,128)(2,1)S(1)}, bf16[64,64]{1,0:T(8,128)(2,1)}, u32[]{:S(2)}) copy-start(bf16[64,64]{1,0:T(8,128)(2,1)} %constant.54.clone) | copy-start | bytes 24580
